TPU v7x, 32 devices: a whole 2x2x4 slice. The times are simulated.
32 devices in a mesh: groups: 2 (over y), rows: 4 (over z), feat: 4 (over x, core).
Axes of the slice: x: 2, y: 2, z: 4, core: 2. Of those that a mesh axis runs over, the one named last changes fastest.
Arguments:
- student: float32 [1280, 4096], P(('groups', 'rows'), 'feat'), parts along dimension 0, may hold values from -1 to 1
- teacher: bfloat16 [1280, 1024], P(('groups', 'rows'), 'feat'), parts along dimension 0, may hold values from -1 to 1
Outputs:
- row_loss: float32 [1280], P(('groups', 'rows')), parts along dimension 0
- student_grad: float32 [1280, 4096], P(('groups', 'rows'), 'feat'), parts along dimension 0
There are 2 independent parts, one for each index of `groups`. A program takes and returns all parts, laid end to end along the dimension named above; each array names one. Nothing has to cross between parts.
All inputs are finite; a program needn't handle non-finite values.
Results may differ from a plain program's by a relative error of at most 0.0085.
Values may be sent and summed in bfloat16 or wider, within the bound.
A program may use at most 64 MiB of HBM per device.

v0:
```python
import jax
import jax.numpy as jnp
from jax import lax
from jax.sharding import PartitionSpec as P

D = 4096
EPSILON = 1e-06


def shifted(block, axis, distance):
    devices = range(lax.axis_size(axis))
    route = [((i - distance) % len(devices), i) for i in devices]
    return lax.ppermute(block, axis, route)


def on_device(student, teacher):
    cycle = lax.axis_size("rows")
    rows_here = student.shape[0]
    width = student.shape[1]
    embeds = rows_here * cycle
    squares = lax.psum(jnp.sum(student * student, axis=1), "feat")
    scaling = lax.rsqrt(squares + EPSILON)
    unit = student * scaling[:, None]
    unit_half = unit.astype(jnp.bfloat16)
    packed = jnp.concatenate([unit_half, teacher], axis=1)
    contract = (((1,), (1,)), ((), ()))

    def absorb(carry, visitor):
        losses, pulled = carry
        other_unit = visitor[:, :width]
        other_teacher = visitor[:, width:]
        student_term = lax.dot_general(
            unit_half, other_unit, contract, preferred_element_type=jnp.float32
        )
        teacher_term = lax.dot_general(
            teacher, other_teacher, contract, preferred_element_type=jnp.float32
        )
        differ = lax.psum((student_term - teacher_term).astype(jnp.bfloat16), "feat").astype(
            jnp.float32
        )
        losses = losses + jnp.sum(differ * differ, axis=1)
        pulled = pulled + jnp.dot(
            differ.astype(jnp.bfloat16), other_unit, preferred_element_type=jnp.float32
        )
        return (losses, pulled)

    carry = (jnp.zeros((rows_here,), jnp.float32), jnp.zeros((rows_here, width), jnp.float32))
    carry = absorb(carry, packed)

    def turn(step, state):
        inner, visitor = state
        visitor = shifted(visitor, "rows", 1)
        return (absorb(inner, visitor), visitor)

    carry, visitor = lax.fori_loop(0, cycle - 1, turn, (carry, packed))
    losses, pulled = carry
    radial = lax.psum(jnp.sum(pulled * unit, axis=1), "feat")
    factor = 4.0 * D / embeds
    student_grad = factor * scaling[:, None] * (pulled - radial[:, None] * unit)
    return (D / embeds * losses, student_grad)


def solution(mesh):
    in_specs = (P(("groups", "rows"), "feat"), P(("groups", "rows"), "feat"))
    out_specs = (P(("groups", "rows")), P(("groups", "rows"), "feat"))
    return jax.shard_map(
        on_device, mesh=mesh, in_specs=in_specs, out_specs=out_specs, check_vma=False
    )
```

profile of v0, /device:TPU:0, one launch (start us, length us, event | category | flops | bytes accessed | tf_op | source)
XLA Modules:
  0.0 104.7 jit_solution(14661461870272374266)
XLA Ops:
  0.6 0.0 copy-start
  0.6 1.3 %multiply_reduce_fusion.2 = f32[160]{0:T(256)S(1)} fusion(f32[160,1024]{1,0:T(8,128)} %param.4), kind=kLoop, calls=%fused_computation.12 | loop fusion | flops 327520 | bytes 656000 | tf_op jit(solution)/shard_map/reduce_sum | solution.py:21
  1.9 8.3 %psum.28 = f32[160]{0:T(256)S(1)} all-reduce(f32[160]{0:T(256)S(1)} %multiply_reduce_fusion.2), channel_id=1, replica_groups=mesh['groups'=2,'rows'=4,'feat'=4] {'feat'}, use_global_device_ids=true, to_apply=%region_1.0 | all-reduce | flops 160 | bytes 1280 | tf_op jit(solution)/shard_map/psum | solution.py:21
  10.3 0.0 copy-done
  10.3 0.0 copy-start.1
  10.3 0.1 multiply_convert_fusion
  10.4 0.8 copy-done.1
  11.2 0.2 fusion.6
  11.3 0.3 fusion.5
  11.6 11.0 %psum.29 = bf16[160,160]{1,0:T(8,128)(2,1)S(1)} all-reduce(bf16[160,160]{1,0:T(8,128)(2,1)S(1)} %fusion.5), channel_id=1, replica_groups=mesh['groups'=2,'rows'=4,'feat'=4] {'feat'}, use_global_device_ids=true, to_apply=%region_2.0 | all-reduce | flops 25600 | bytes 102400 | tf_op jit(solution)/shard_map/psum | solution.py:38
  22.6 0.2 fusion.7
  22.8 0.1 multiply_reduce_fusion.3
  23.0 74.0 %while.14 = (s32[]{:T(128)}, f32[160]{0:T(256)S(1)}, f32[160,1024]{1,0:T(8,128)S(1)}, bf16[160,1280]{1,0:T(8,128)(2,1)S(1)}, bf16[160,1024]{1,0:T(8,128)(2,1)S(1)}, /*index=5*/bf16[160,256]{1,0:T(8,128)(2,1)S(1)}, s32[]{:T(128)}) while((s32[]{:T(128)}, f32[160]{0:T(256)S(1)}, f32[160,1024]{1,0:T(8,128)S(1)}, bf16[160,1280]{1,0:T(8,128)(2,1)S(1)}, ...), condition=%wide.region_7.0_spmd, body=%wide.region_4.0_spmd.sunk | while | flops 118282240 | bytes 5470837 | solution.py:55
  23.0 1.8 %collective-permute-start = (bf16[160,1280]{1,0:T(8,128)(2,1)S(1)}, bf16[160,1280]{1,0:T(8,128)(2,1)S(1)}, u32[]{:S(2)}, u32[]{:S(2)}) collective-permute-start(bf16[160,1280]{1,0:T(8,128)(2,1)S(1)} %get-tuple-element.98), channel_id=1, source_target_pairs={{12,0},{0,4},{4,8},{8,12},{13,1},{1,5},{5,9},{9,13},{14,2},{2,6},{... | collective-permute-start | bytes 1228808 | tf_op jit(solution)/shard_map/while/body/eval_jaxpr/ppermute | solution.py:13
  24.9 11.0 %collective-permute-done = bf16[160,1280]{1,0:T(8,128)(2,1)S(1)} collective-permute-done((bf16[160,1280]{1,0:T(8,128)(2,1)S(1)}, bf16[160,1280]{1,0:T(8,128)(2,1)S(1)}, u32[]{:S(2)}, u32[]{:S(2)}) %collective-permute-start) | collective-permute-done | bytes 409632 | tf_op jit(solution)/shard_map/while/body/eval_jaxpr/ppermute | solution.py:13
  35.9 0.2 fusion.31
  36.1 0.3 fusion.32
  36.3 11.0 %psum.32 = bf16[160,160]{1,0:T(8,128)(2,1)S(1)} all-reduce(bf16[160,160]{1,0:T(8,128)(2,1)S(1)} %fusion.32), channel_id=1, replica_groups=mesh['groups'=2,'rows'=4,'feat'=4] {'feat'}, use_global_device_ids=true, to_apply=%region_5.0 | all-reduce | flops 25600 | bytes 102400 | tf_op jit(solution)/shard_map/while/body/eval_jaxpr/psum | solution.py:38
  47.3 0.1 multiply_reduce_fusion.5
  47.5 0.2 convolution_add_fusion.2
  47.8 0.1 collective-permute-start
  47.8 12.7 %collective-permute-done = bf16[160,1280]{1,0:T(8,128)(2,1)S(1)} collective-permute-done((bf16[160,1280]{1,0:T(8,128)(2,1)S(1)}, bf16[160,1280]{1,0:T(8,128)(2,1)S(1)}, u32[]{:S(2)}, u32[]{:S(2)}) %collective-permute-start) | collective-permute-done | bytes 409632 | tf_op jit(solution)/shard_map/while/body/eval_jaxpr/ppermute | solution.py:13
  60.5 0.2 fusion.31
  60.7 0.3 fusion.32
  61.0 10.9 %psum.32 = bf16[160,160]{1,0:T(8,128)(2,1)S(1)} all-reduce(bf16[160,160]{1,0:T(8,128)(2,1)S(1)} %fusion.32), channel_id=1, replica_groups=mesh['groups'=2,'rows'=4,'feat'=4] {'feat'}, use_global_device_ids=true, to_apply=%region_5.0 | all-reduce | flops 25600 | bytes 102400 | tf_op jit(solution)/shard_map/while/body/eval_jaxpr/psum | solution.py:38
  71.9 0.1 multiply_reduce_fusion.5
  72.1 0.2 convolution_add_fusion.2
  72.3 0.1 collective-permute-start
  72.4 12.8 %collective-permute-done = bf16[160,1280]{1,0:T(8,128)(2,1)S(1)} collective-permute-done((bf16[160,1280]{1,0:T(8,128)(2,1)S(1)}, bf16[160,1280]{1,0:T(8,128)(2,1)S(1)}, u32[]{:S(2)}, u32[]{:S(2)}) %collective-permute-start) | collective-permute-done | bytes 409632 | tf_op jit(solution)/shard_map/while/body/eval_jaxpr/ppermute | solution.py:13
  85.2 0.2 fusion.31
  85.4 0.3 fusion.32
  85.7 10.9 %psum.32 = bf16[160,160]{1,0:T(8,128)(2,1)S(1)} all-reduce(bf16[160,160]{1,0:T(8,128)(2,1)S(1)} %fusion.32), channel_id=1, replica_groups=mesh['groups'=2,'rows'=4,'feat'=4] {'feat'}, use_global_device_ids=true, to_apply=%region_5.0 | all-reduce | flops 25600 | bytes 102400 | tf_op jit(solution)/shard_map/while/body/eval_jaxpr/psum | solution.py:38
  96.6 0.1 multiply_reduce_fusion.5
  96.7 0.2 convolution_add_fusion.2
  97.0 0.2 multiply_reduce_fusion.1
  97.2 5.9 %psum.30 = f32[160]{0:T(256)S(1)} all-reduce(f32[160]{0:T(256)S(1)} %multiply_reduce_fusion.1), channel_id=1, replica_groups=mesh['groups'=2,'rows'=4,'feat'=4] {'feat'}, use_global_device_ids=true, to_apply=%region_9.0 | all-reduce | flops 160 | bytes 1280 | tf_op jit(solution)/shard_map/psum | solution.py:57
  103.1 1.0 subtract_multiply_fusion
  104.1 0.6 broadcast_multiply_fusion.1
  (8 shorter events, 0.2 us)
Async XLA Ops:
  0.6 9.6 %copy-start = (f32[160,1024]{1,0:T(8,128)S(1)}, f32[160,1024]{1,0:T(8,128)}, u32[]{:S(2)}) copy-start(f32[160,1024]{1,0:T(8,128)} %param.4) | copy-start | bytes 1966084
  10.3 0.9 copy-start.1
  23.0 12.9 %collective-permute-start = (bf16[160,1280]{1,0:T(8,128)(2,1)S(1)}, bf16[160,1280]{1,0:T(8,128)(2,1)S(1)}, u32[]{:S(2)}, u32[]{:S(2)}) collective-permute-start(bf16[160,1280]{1,0:T(8,128)(2,1)S(1)} %get-tuple-element.98), channel_id=1, source_target_pairs={{12,0},{0,4},{4,8},{8,12},{13,1},{1,5},{5,9},{9,13},{14,2},{2,6},{... | collective-permute-start | bytes 1228808 | tf_op jit(solution)/shard_map/while/body/eval_jaxpr/ppermute | solution.py:13
  47.8 12.8 %collective-permute-start = (bf16[160,1280]{1,0:T(8,128)(2,1)S(1)}, bf16[160,1280]{1,0:T(8,128)(2,1)S(1)}, u32[]{:S(2)}, u32[]{:S(2)}) collective-permute-start(bf16[160,1280]{1,0:T(8,128)(2,1)S(1)} %get-tuple-element.98), channel_id=1, source_target_pairs={{12,0},{0,4},{4,8},{8,12},{13,1},{1,5},{5,9},{9,13},{14,2},{2,6},{... | collective-permute-start | bytes 1228808 | tf_op jit(solution)/shard_map/while/body/eval_jaxpr/ppermute | solution.py:13
  72.3 12.9 %collective-permute-start = (bf16[160,1280]{1,0:T(8,128)(2,1)S(1)}, bf16[160,1280]{1,0:T(8,128)(2,1)S(1)}, u32[]{:S(2)}, u32[]{:S(2)}) collective-permute-start(bf16[160,1280]{1,0:T(8,128)(2,1)S(1)} %get-tuple-element.98), channel_id=1, source_target_pairs={{12,0},{0,4},{4,8},{8,12},{13,1},{1,5},{5,9},{9,13},{14,2},{2,6},{... | collective-permute-start | bytes 1228808 | tf_op jit(solution)/shard_map/while/body/eval_jaxpr/ppermute | solution.py:13
where the time goes:
time: 105 us
  blocking collectives  58.1 us (55%)
  waiting for transfers between devices  36.5 us (35%)
  other arithmetic  3.7 us (4%)
  matrix products  2.71 us (3%)
  starting transfers between devices  1.96 us (2%)
    psum x4, blocking collectives, absorb(): lax.psum((student_term - teacher_term).astype(jnp.bfloat16), 'feat')  43.8 us
    ppermute x3, waiting for transfers between devices, shifted(): return lax.ppermute(block, axis, route)  36.5 us
    psum x1, blocking collectives, on_device(): squares = lax.psum(jnp.sum(student * student, axis=1), 'feat')  8.34 us
    psum x1, blocking collectives, on_device(): radial = lax.psum(jnp.sum(pulled * unit, axis=1), 'feat')  5.89 us
  transfers between devices with their start and end apart: 3, of which 3 were waited for; matrix products, arithmetic and copies ran while one was open for 0% of the time, Pallas kernels for 0%

commit v1 on v0

--- a/solution.py
+++ b/solution.py
@@ -18,7 +18,7 @@
     rows_here = student.shape[0]
     width = student.shape[1]
     embeds = rows_here * cycle
-    squares = lax.psum(jnp.sum(student * student, axis=1), "feat")
+    squares = jnp.sum(lax.all_gather(jnp.sum(student * student, axis=1), "feat"), axis=0)
     scaling = lax.rsqrt(squares + EPSILON)
     unit = student * scaling[:, None]
     unit_half = unit.astype(jnp.bfloat16)

time: 105 us -> 107 us (1.019)
  local copies, waits for them, and re-layouts: 0.87 us -> 2.41 us
    psum x1 -> x0, blocking collectives: 8.34 us -> none  [on_device(): squares = lax.psum(jnp.sum(student * student, axis=1), 'feat')]
    unnamed x0 -> x1, blocking collectives: none -> 8.31 us
    unnamed x4 -> x9, local copies, waits for them, and re-layouts: 0.78 us -> 2.24 us
where the time goes in v1:
time: 107 us
  blocking collectives  58.1 us (54%)
  waiting for transfers between devices  36.5 us (34%)
  other arithmetic  3.66 us (3%)
  matrix products  2.71 us (3%)
  local copies, waits for them, and re-layouts  2.41 us (2%)
  starting transfers between devices  1.96 us (2%)
  between operations  1.39 us (1%)
    psum x4, blocking collectives, absorb(): lax.psum((student_term - teacher_term).astype(jnp.bfloat16), 'feat')  43.9 us
    ppermute x3, waiting for transfers between devices, shifted(): return lax.ppermute(block, axis, route)  36.5 us
    unnamed x1, blocking collectives  8.31 us
    psum x1, blocking collectives, on_device(): radial = lax.psum(jnp.sum(pulled * unit, axis=1), 'feat')  5.91 us
    unnamed x9, local copies, waits for them, and re-layouts  2.24 us
  transfers between devices with their start and end apart: 3, of which 3 were waited for; matrix products, arithmetic and copies ran while one was open for 0% of the time, Pallas kernels for 0%

profile of v1, /device:TPU:0, one launch (start us, length us, event | category | flops | bytes accessed | tf_op | source)
XLA Modules:
  0.0 106.9 jit_solution(12869327582182654565)
XLA Ops:
  0.6 0.0 copy-start.2
  0.6 0.0 copy-start
  0.7 0.6 copy-done.2
  1.3 0.6 dynamic-slice
  2.5 1.2 %multiply_reduce_fusion.2 = f32[160]{0:T(256)S(1)} fusion(f32[160,1024]{1,0:T(8,128)} %param.4), kind=kLoop, calls=%fused_computation.12 | loop fusion | flops 327520 | bytes 656000 | tf_op jit(solution)/shard_map/reduce_sum | solution.py:21
  3.7 0.2 dynamic-update-slice
  4.0 8.3 %all-reduce = f32[640]{0:T(1024)S(1)} all-reduce(f32[640]{0:T(1024)S(1)} %dynamic-update-slice), channel_id=2, replica_groups=mesh['groups'=2,'rows'=4,'feat'=4] {'feat'}, use_global_device_ids=true, to_apply=%add | all-reduce | flops 640 | bytes 5120
  12.3 0.1 reshape.13
  12.4 0.0 copy-done
  12.4 0.0 copy-start.1
  12.4 0.1 multiply_convert_fusion
  12.6 0.8 copy-done.1
  13.3 0.2 fusion.6
  13.5 0.3 fusion.5
  13.8 11.0 %psum.21 = bf16[160,160]{1,0:T(8,128)(2,1)S(1)} all-reduce(bf16[160,160]{1,0:T(8,128)(2,1)S(1)} %fusion.5), channel_id=1, replica_groups=mesh['groups'=2,'rows'=4,'feat'=4] {'feat'}, use_global_device_ids=true, to_apply=%region_2.0 | all-reduce | flops 25600 | bytes 102400 | tf_op jit(solution)/shard_map/psum | solution.py:38
  24.8 0.2 fusion.7
  25.0 0.1 multiply_reduce_fusion.3
  25.2 74.0 %while.14 = (s32[]{:T(128)}, f32[160]{0:T(256)S(1)}, f32[160,1024]{1,0:T(8,128)S(1)}, bf16[160,1280]{1,0:T(8,128)(2,1)S(1)}, bf16[160,1024]{1,0:T(8,128)(2,1)S(1)}, /*index=5*/bf16[160,256]{1,0:T(8,128)(2,1)S(1)}, s32[]{:T(128)}) while((s32[]{:T(128)}, f32[160]{0:T(256)S(1)}, f32[160,1024]{1,0:T(8,128)S(1)}, bf16[160,1280]{1,0:T(8,128)(2,1)S(1)}, ...), condition=%wide.region_7.0_spmd, body=%wide.region_4.0_spmd.sunk | while | flops 118282240 | bytes 5470837 | solution.py:55
  25.2 1.8 %collective-permute-start = (bf16[160,1280]{1,0:T(8,128)(2,1)S(1)}, bf16[160,1280]{1,0:T(8,128)(2,1)S(1)}, u32[]{:S(2)}, u32[]{:S(2)}) collective-permute-start(bf16[160,1280]{1,0:T(8,128)(2,1)S(1)} %get-tuple-element.98), channel_id=1, source_target_pairs={{12,0},{0,4},{4,8},{8,12},{13,1},{1,5},{5,9},{9,13},{14,2},{2,6},{... | collective-permute-start | bytes 1228808 | tf_op jit(solution)/shard_map/while/body/eval_jaxpr/ppermute | solution.py:13
  27.0 11.0 %collective-permute-done = bf16[160,1280]{1,0:T(8,128)(2,1)S(1)} collective-permute-done((bf16[160,1280]{1,0:T(8,128)(2,1)S(1)}, bf16[160,1280]{1,0:T(8,128)(2,1)S(1)}, u32[]{:S(2)}, u32[]{:S(2)}) %collective-permute-start) | collective-permute-done | bytes 409632 | tf_op jit(solution)/shard_map/while/body/eval_jaxpr/ppermute | solution.py:13
  38.0 0.2 fusion.31
  38.2 0.3 fusion.32
  38.5 11.0 %psum.24 = bf16[160,160]{1,0:T(8,128)(2,1)S(1)} all-reduce(bf16[160,160]{1,0:T(8,128)(2,1)S(1)} %fusion.32), channel_id=1, replica_groups=mesh['groups'=2,'rows'=4,'feat'=4] {'feat'}, use_global_device_ids=true, to_apply=%region_5.0 | all-reduce | flops 25600 | bytes 102400 | tf_op jit(solution)/shard_map/while/body/eval_jaxpr/psum | solution.py:38
  49.5 0.1 multiply_reduce_fusion.5
  49.7 0.2 convolution_add_fusion.2
  50.0 0.1 collective-permute-start
  50.0 12.7 %collective-permute-done = bf16[160,1280]{1,0:T(8,128)(2,1)S(1)} collective-permute-done((bf16[160,1280]{1,0:T(8,128)(2,1)S(1)}, bf16[160,1280]{1,0:T(8,128)(2,1)S(1)}, u32[]{:S(2)}, u32[]{:S(2)}) %collective-permute-start) | collective-permute-done | bytes 409632 | tf_op jit(solution)/shard_map/while/body/eval_jaxpr/ppermute | solution.py:13
  62.7 0.2 fusion.31
  62.9 0.3 fusion.32
  63.1 10.9 %psum.24 = bf16[160,160]{1,0:T(8,128)(2,1)S(1)} all-reduce(bf16[160,160]{1,0:T(8,128)(2,1)S(1)} %fusion.32), channel_id=1, replica_groups=mesh['groups'=2,'rows'=4,'feat'=4] {'feat'}, use_global_device_ids=true, to_apply=%region_5.0 | all-reduce | flops 25600 | bytes 102400 | tf_op jit(solution)/shard_map/while/body/eval_jaxpr/psum | solution.py:38
  74.1 0.1 multiply_reduce_fusion.5
  74.2 0.2 convolution_add_fusion.2
  74.5 0.1 collective-permute-start
  74.6 12.8 %collective-permute-done = bf16[160,1280]{1,0:T(8,128)(2,1)S(1)} collective-permute-done((bf16[160,1280]{1,0:T(8,128)(2,1)S(1)}, bf16[160,1280]{1,0:T(8,128)(2,1)S(1)}, u32[]{:S(2)}, u32[]{:S(2)}) %collective-permute-start) | collective-permute-done | bytes 409632 | tf_op jit(solution)/shard_map/while/body/eval_jaxpr/ppermute | solution.py:13
  87.3 0.2 fusion.31
  87.5 0.3 fusion.32
  87.8 10.9 %psum.24 = bf16[160,160]{1,0:T(8,128)(2,1)S(1)} all-reduce(bf16[160,160]{1,0:T(8,128)(2,1)S(1)} %fusion.32), channel_id=1, replica_groups=mesh['groups'=2,'rows'=4,'feat'=4] {'feat'}, use_global_device_ids=true, to_apply=%region_5.0 | all-reduce | flops 25600 | bytes 102400 | tf_op jit(solution)/shard_map/while/body/eval_jaxpr/psum | solution.py:38
  98.7 0.1 multiply_reduce_fusion.5
  98.9 0.2 convolution_add_fusion.2
  99.1 0.2 multiply_reduce_fusion.1
  99.4 5.9 %psum.22 = f32[160]{0:T(256)S(1)} all-reduce(f32[160]{0:T(256)S(1)} %multiply_reduce_fusion.1), channel_id=1, replica_groups=mesh['groups'=2,'rows'=4,'feat'=4] {'feat'}, use_global_device_ids=true, to_apply=%region_9.0 | all-reduce | flops 160 | bytes 1280 | tf_op jit(solution)/shard_map/psum | solution.py:57
  105.3 1.0 subtract_multiply_fusion
  106.3 0.6 broadcast_multiply_fusion.1
  (10 shorter events, 0.2 us)
Async XLA Ops:
  0.6 0.7 copy-start.2
  0.6 11.8 %copy-start = (f32[160,1024]{1,0:T(8,128)S(1)}, f32[160,1024]{1,0:T(8,128)}, u32[]{:S(2)}) copy-start(f32[160,1024]{1,0:T(8,128)} %param.4) | copy-start | bytes 1966084
  12.4 0.9 copy-start.1
  25.2 12.8 %collective-permute-start = (bf16[160,1280]{1,0:T(8,128)(2,1)S(1)}, bf16[160,1280]{1,0:T(8,128)(2,1)S(1)}, u32[]{:S(2)}, u32[]{:S(2)}) collective-permute-start(bf16[160,1280]{1,0:T(8,128)(2,1)S(1)} %get-tuple-element.98), channel_id=1, source_target_pairs={{12,0},{0,4},{4,8},{8,12},{13,1},{1,5},{5,9},{9,13},{14,2},{2,6},{... | collective-permute-start | bytes 1228808 | tf_op jit(solution)/shard_map/while/body/eval_jaxpr/ppermute | solution.py:13
  50.0 12.7 %collective-permute-start = (bf16[160,1280]{1,0:T(8,128)(2,1)S(1)}, bf16[160,1280]{1,0:T(8,128)(2,1)S(1)}, u32[]{:S(2)}, u32[]{:S(2)}) collective-permute-start(bf16[160,1280]{1,0:T(8,128)(2,1)S(1)} %get-tuple-element.98), channel_id=1, source_target_pairs={{12,0},{0,4},{4,8},{8,12},{13,1},{1,5},{5,9},{9,13},{14,2},{2,6},{... | collective-permute-start | bytes 1228808 | tf_op jit(solution)/shard_map/while/body/eval_jaxpr/ppermute | solution.py:13
  74.5 12.9 %collective-permute-start = (bf16[160,1280]{1,0:T(8,128)(2,1)S(1)}, bf16[160,1280]{1,0:T(8,128)(2,1)S(1)}, u32[]{:S(2)}, u32[]{:S(2)}) collective-permute-start(bf16[160,1280]{1,0:T(8,128)(2,1)S(1)} %get-tuple-element.98), channel_id=1, source_target_pairs={{12,0},{0,4},{4,8},{8,12},{13,1},{1,5},{5,9},{9,13},{14,2},{2,6},{... | collective-permute-start | bytes 1228808 | tf_op jit(solution)/shard_map/while/body/eval_jaxpr/ppermute | solution.py:13
